TPU v7x, 256 devices: a whole 4x4x8 slice. The times are simulated.
256 devices in a mesh: row: 32 (over x, z), col: 8 (over y, core).
Axes of the slice: x: 4, y: 4, z: 8, core: 2. Of those that a mesh axis runs over, the one named last changes fastest.
Arguments:
- latent: bfloat16 [1024, 1024, 128], P('row', 'col'), may hold values from -140 to 140
- group_norm_gain: float32 [128], replicated, may hold values from 0.25 to 1.75
- group_norm_bias: float32 [128], replicated, may hold values from -2.5 to 2.5
- decoder_weight: bfloat16 [3, 3, 128, 3], replicated, may hold values from -0.1875 to 0.1875
- decoder_bias: float32 [3], replicated, may hold values from -2.5 to 2.5
- first_weight: bfloat16 [3, 3, 3, 64], replicated, may hold values from -1.25 to 1.25
- first_bias: float32 [64], replicated, may hold values from -2.5 to 2.5
- second_weight: bfloat16 [3, 3, 64, 64], replicated, may hold values from -0.25 to 0.25
- second_bias: float32 [64], replicated, may hold values from -2.5 to 2.5
- third_weight: bfloat16 [3, 3, 64, 128], replicated, may hold values from -0.25 to 0.25
- third_bias: float32 [128], replicated, may hold values from -2.5 to 2.5
- fourth_weight: bfloat16 [3, 3, 128, 128], replicated, may hold values from -0.1875 to 0.1875
- fourth_bias: float32 [128], replicated, may hold values from -2.5 to 2.5
- exemplar_low: float32 [64, 64], replicated, may hold values from -1.2 to 1.2
- exemplar_high: float32 [128, 128], replicated, may hold values from -1.2 to 1.2
Outputs:
- latent_grad: bfloat16 [1024, 1024, 128], P('row', 'col')
- style_loss: float32 [], replicated
All inputs are finite; a program needn't handle non-finite values.
Results may differ from a plain program's by a relative error of at most 0.014.
Values may be sent and summed in bfloat16 or wider, within the bound.
No kernel may reach another device: no remote copies, remote signals or barrier semaphores. Data moves between devices by JAX's collectives and lax.ppermute only.
A program may use at most 64 MiB of HBM per device.

v0:
```python
import jax
import jax.numpy as jnp
from jax import lax
from jax.sharding import PartitionSpec as P

GROUPS = 32


eps_norm = 1e-05
pix_mean = (0.485, 0.456, 0.406)
pix_std = (0.229, 0.224, 0.225)


def extended(value, sides, width):
    for axis, dim in sides:
        count, length = (lax.axis_size(axis), value.shape[dim])
        up = [(i, (i + 1) % count) for i in range(count - 1)]
        down = [(j, i) for i, j in up]
        last = lax.slice_in_dim(value, length - width, length, axis=dim)
        leading = lax.slice_in_dim(value, 0, width, axis=dim)
        before = lax.ppermute(last, axis, up)
        after = lax.ppermute(leading, axis, down)
        value = jnp.concatenate([before, value, after], axis=dim)
    return value


def gelu_value(pre):
    return pre * 0.5 * (1.0 + lax.erf(pre * 0.7071067811865476))


def gelu_slope(pre):
    return (
        0.5 * (1.0 + lax.erf(pre * 0.7071067811865476))
        + pre * jnp.exp(-0.5 * pre * pre) * 0.3989422804014327
    )


def silu_slope(value):
    sig = jax.nn.sigmoid(value)
    return sig * (1.0 + value * (1.0 - sig))


def conv_valid(padded, kernel):
    return lax.conv_general_dilated(
        padded[None],
        kernel,
        (1, 1),
        "VALID",
        dimension_numbers=("NHWC", "HWIO", "NHWC"),
        preferred_element_type=jnp.float32,
    )[0]


def with_rim(source):
    return extended(source, (("row", 0), ("col", 1)), 1)


def conv_forward(source, kernel):
    return conv_valid(with_rim(source), kernel)


def conv_back(source, kernel):
    return conv_valid(with_rim(source), jnp.transpose(kernel[::-1, ::-1], (0, 1, 3, 2)))


def gram_part(feature):
    flat = feature.reshape(-1, feature.shape[-1])
    return lax.dot_general(flat, flat, (((0,), (0,)), ((), ())), preferred_element_type=jnp.float32)


def times_sym(flat, sym):
    sym_upper = sym.astype(jnp.bfloat16)
    sym_lower = (sym - sym_upper.astype(jnp.float32)).astype(jnp.bfloat16)
    return jnp.dot(flat, sym_upper, preferred_element_type=jnp.float32) + jnp.dot(
        flat, sym_lower, preferred_element_type=jnp.float32
    )


def local(
    latent,
    group_norm_gain,
    group_norm_bias,
    decoder_weight,
    decoder_bias,
    first_weight,
    first_bias,
    second_weight,
    second_bias,
    third_weight,
    third_bias,
    fourth_weight,
    fourth_bias,
    exemplar_low,
    exemplar_high,
):
    patch_rows, patch_columns, channel_count = latent.shape
    low_chans = first_weight.shape[3]
    high_chans = third_weight.shape[3]
    npix = patch_rows * patch_columns * lax.axis_size("row") * lax.axis_size("col")
    group_view = latent.astype(jnp.float32).reshape(
        patch_rows * patch_columns, GROUPS, channel_count // GROUPS
    )
    element_count = npix * (channel_count // GROUPS)
    sums, squares = lax.psum(
        (jnp.sum(group_view, axis=(0, 2)), jnp.sum(group_view * group_view, axis=(0, 2))),
        ("row", "col"),
    )
    group_mean = sums / element_count
    msq_g = squares / element_count
    inverse_deviation = 1.0 / jnp.sqrt(msq_g - group_mean * group_mean + eps_norm)
    normed_input = (group_view - group_mean[None, :, None]) * inverse_deviation[None, :, None]
    before_norm_input = (
        group_norm_gain * normed_input.reshape(patch_rows, patch_columns, channel_count)
        + group_norm_bias
    )
    activated = jax.nn.silu(before_norm_input).astype(jnp.bfloat16)
    padded = extended(activated, (("row", 0), ("col", 1)), 1)
    rgb = conv_valid(padded, decoder_weight) + decoder_bias
    color_mean = jnp.array(pix_mean, jnp.float32)
    color_std = jnp.array(pix_std, jnp.float32)
    pixels = (((rgb + 1.0) * 0.5 - color_mean) / color_std).astype(jnp.bfloat16)
    pre_one = conv_forward(pixels, first_weight) + first_bias
    feat_one = gelu_value(pre_one).astype(jnp.bfloat16)
    pre_two = conv_forward(feat_one, second_weight) + second_bias
    feat_two = gelu_value(pre_two).astype(jnp.bfloat16)
    part_low = gram_part(feat_two)
    pooled = feat_two.astype(jnp.float32).reshape(
        patch_rows // 2, 2, patch_columns // 2, 2, low_chans
    )
    pooled = pooled.mean(axis=(1, 3)).astype(jnp.bfloat16)
    pre_three = conv_forward(pooled, third_weight) + third_bias
    feat_three = gelu_value(pre_three).astype(jnp.bfloat16)
    pre_four = conv_forward(feat_three, fourth_weight) + fourth_bias
    feat_four = gelu_value(pre_four).astype(jnp.bfloat16)
    part_high = gram_part(feat_four)
    total_low, total_high = lax.psum((part_low, part_high), ("row", "col"))
    gap_low = total_low / npix - exemplar_low
    gap_high = total_high / (npix // 4) - exemplar_high
    sym_low = gap_low + gap_low.T
    sym_high = gap_high + gap_high.T
    style_loss = jnp.sum(gap_low * gap_low) / (low_chans * low_chans) + jnp.sum(
        gap_high * gap_high
    ) / (high_chans * high_chans)
    grad_four = 2.0 * times_sym(feat_four.reshape(-1, high_chans), sym_high).reshape(
        patch_rows // 2, patch_columns // 2, high_chans
    )
    back_four = (grad_four * gelu_slope(pre_four)).astype(jnp.bfloat16)
    back_three = (conv_back(back_four, fourth_weight) * gelu_slope(pre_three)).astype(jnp.bfloat16)
    grad_pool = conv_back(back_three, third_weight)
    spread = jnp.repeat(jnp.repeat(grad_pool, 2, axis=0), 2, axis=1) * 0.25
    gram_term = 2.0 * times_sym(feat_two.reshape(-1, low_chans), sym_low).reshape(
        patch_rows, patch_columns, low_chans
    )
    back_two = ((spread + gram_term) * gelu_slope(pre_two)).astype(jnp.bfloat16)
    back_one = (conv_back(back_two, second_weight) * gelu_slope(pre_one)).astype(jnp.bfloat16)
    back_rgb = (conv_back(back_one, first_weight) * (0.5 / color_std)).astype(jnp.bfloat16)
    grad_act = conv_back(back_rgb, decoder_weight)
    dxhat = grad_act * silu_slope(before_norm_input) * group_norm_gain
    group_view_gradient = dxhat.reshape(patch_rows * patch_columns, GROUPS, channel_count // GROUPS)
    first_sum, second_sum = lax.psum(
        (
            jnp.sum(group_view_gradient, axis=(0, 2)),
            jnp.sum(group_view_gradient * normed_input, axis=(0, 2)),
        ),
        ("row", "col"),
    )
    mean_first_pass = first_sum / element_count
    mean_second_pass = second_sum / element_count
    step_output = inverse_deviation[None, :, None] * (
        group_view_gradient
        - mean_first_pass[None, :, None]
        - normed_input * mean_second_pass[None, :, None]
    )
    return (
        step_output.reshape(patch_rows, patch_columns, channel_count).astype(jnp.bfloat16),
        style_loss,
    )


def solution(mesh):
    placed = (
        P("row", "col", None),
        P(),
        P(),
        P(),
        P(),
        P(),
        P(),
        P(),
        P(),
        P(),
        P(),
        P(),
        P(),
        P(),
        P(),
    )
    return jax.shard_map(
        local, mesh=mesh, in_specs=placed, out_specs=(P("row", "col", None), P()), check_vma=False
    )
```

profile of v0, /device:TPU:1, one launch (start us, length us, event | category | flops | bytes accessed | tf_op | source)
XLA Modules:
  0.0 756.9 jit_solution(5666820437561833054)
XLA Ops:
  9.5 81.4 %all-reduce.1 = (f32[32]{0:T(128)S(1)}, f32[32]{0:T(128)S(1)}) all-reduce(f32[32]{0:T(128)S(1)} %reduce_sum.96, f32[32]{0:T(128)S(1)} %reduce_sum.75), channel_id=1, replica_groups=mesh['row'=32,'col'=8] {'row','col'}, use_global_device_ids=true, to_apply=%region_5.6 | all-reduce | flops 64 | bytes 512 | tf_op jit(solution)/shard_map/psum | solution.py:104
  97.5 3.7 collective-permute-done.1
  101.2 3.2 collective-permute-start.2
  111.2 24.5 %fusion.73 = f32[32,8,17,3]{1,3,2,0:T(4,128)S(1)} fusion(bf16[3,3,128,3]{2,3,1,0:T(4,128)(2,1)S(1)} %copy-done.26, bf16[34,1,7,2,128]{4,2,3,0,1:T(8,128)(2,1)S(1)} %slice.184, bf16[34,1,8,17,128]{4,2,3,0,1:T(8,128)(2,1)S(1)} %copy.289, pred[8,17]{0,1:T(8,128)(4,1)S(1)} %copy-done.27), kind=kOutput, calls=%fused_computation.101 | convolution fusion | flops 34063104 | bytes 1364872 | tf_op jit(solution)/shard_map/conv_general_dilated | solution.py:44
  139.6 3.3 collective-permute-done.5
  155.7 4.0 collective-permute-start.8
  161.1 4.0 collective-permute-done.9
  181.5 3.7 collective-permute-start.12
  186.5 3.6 collective-permute-done.13
  190.0 3.1 collective-permute-start.14
  199.5 3.6 collective-permute-start.16
  207.8 3.4 collective-permute-start.18
  220.1 242.3 %all-reduce.4.cloned.1.call-done = f32[128,128]{1,0:T(8,128)} async-done(((f32[128,128]{1,0:T(8,128)}), f32[128,128]{1,0:T(8,128)}) %all-reduce.4.cloned.1.call-update) | async-done | bytes 65552 | tf_op jit(solution)/shard_map/psum | solution.py:136
  464.9 3.6 collective-permute-start.20
  470.1 77.1 %psum.45 = f32[64,64]{1,0:T(8,128)S(1)} all-reduce(f32[64,64]{1,0:T(8,128)S(1)} %convolution_bitcast_fusion.1), channel_id=1, replica_groups=mesh['row'=32,'col'=8] {'row','col'}, use_global_device_ids=true, to_apply=%region_8.9 | all-reduce | flops 4096 | bytes 32768 | tf_op jit(solution)/shard_map/psum | solution.py:136
  555.8 3.7 collective-permute-start.24
  564.2 3.4 collective-permute-start.26
  579.6 3.8 collective-permute-done.29
  583.5 4.9 collective-permute-start.30
  604.6 3.7 collective-permute-done.33
  608.4 3.4 collective-permute-start.34
  618.0 24.5 %fusion.70 = f32[32,8,17,3]{1,3,2,0:T(4,128)S(1)} fusion(bf16[3,3,3,64]{3,2,1,0:T(4,128)(2,1)S(1)} %copy-done.25, bf16[34,1,7,2,64]{4,2,3,0,1:T(8,128)(2,1)S(1)} %slice.220, bf16[34,1,8,17,64]{4,2,3,0,1:T(8,128)(2,1)S(1)} %copy.328, pred[8,17]{0,1:T(8,128)(4,1)S(1)} %copy-done.27), kind=kOutput, calls=%fused_computation.100 | convolution fusion | flops 17038080 | bytes 708616 | tf_op jit(solution)/shard_map/conv_general_dilated | solution.py:44
  651.0 3.3 collective-permute-start.38
  665.9 80.2 %all-reduce = (f32[32]{0:T(128)S(1)}, f32[32]{0:T(128)S(1)}) all-reduce(f32[32]{0:T(128)S(1)} %reduce_sum.103, f32[32]{0:T(128)S(1)} %reduce_sum.100), channel_id=1, replica_groups=mesh['row'=32,'col'=8] {'row','col'}, use_global_device_ids=true, to_apply=%region_14.15 | all-reduce | flops 64 | bytes 512 | tf_op jit(solution)/shard_map/psum | solution.py:160
  (265 shorter events, 143.3 us)
Async XLA Ops:
  7.2 455.2 %all-reduce.4.cloned.1.call-start = ((), (), s32[]{:S(2)}) async-start(), calls=%async_computation | async-start | bytes 131072 | tf_op jit(solution)/shard_map/psum | solution.py:136
  96.2 5.0 collective-permute-start.1
  101.2 5.7 collective-permute-start.2
  143.0 5.2 collective-permute-start.6
  146.1 5.2 collective-permute-start.7
  155.7 5.3 collective-permute-start.8
  159.8 5.3 collective-permute-start.9
  165.1 5.0 collective-permute-start.10
  190.0 5.0 collective-permute-start.14
  199.5 7.9 %collective-permute-start.16 = (bf16[1,64,128]{2,0,1:T(2,128)(2,1)S(1)}, bf16[1,64,128]{2,0,1:T(2,128)(2,1)S(1)}, u32[]{:S(2)}, u32[]{:S(2)}) collective-permute-start(bf16[1,64,128]{2,0,1:T(2,128)(2,1)S(1)} %get-tuple-element.55), channel_id=1, source_target_pairs={{0,8},{8,16},{16,24},{24,32},{32,40},{40,48},{48,56},{56,64},{64,7... | collective-permute-start | bytes 49160 | tf_op jit(solution)/shard_map/ppermute | solution.py:21
  207.8 9.5 %collective-permute-start.18 = (bf16[18,1,128]{2,0,1:T(8,128)(2,1)S(1)}, bf16[18,1,128]{2,0,1:T(8,128)(2,1)S(1)}, u32[]{:S(2)}, u32[]{:S(2)}) collective-permute-start(bf16[18,1,128]{2,0,1:T(8,128)(2,1)S(1)} %get-tuple-element.47), channel_id=1, source_target_pairs={{0,1},{1,2},{2,3},{3,4},{4,5},{5,6},{6,7},{8,9},{9,10},{10,11},{11... | collective-permute-start | bytes 13832 | tf_op jit(solution)/shard_map/ppermute | solution.py:21
  211.2 6.1 collective-permute-start.19
  464.9 82.4 %collective-permute-start.20 = (bf16[1,64,128]{2,0,1:T(2,128)(2,1)S(1)}, bf16[1,64,128]{2,0,1:T(2,128)(2,1)S(1)}, u32[]{:S(2)}, u32[]{:S(2)}) collective-permute-start(bf16[1,64,128]{2,0,1:T(2,128)(2,1)S(1)} %get-tuple-element.53), channel_id=1, source_target_pairs={{0,8},{8,16},{16,24},{24,32},{32,40},{40,48},{48,56},{56,64},{64,7... | collective-permute-start | bytes 49160 | tf_op jit(solution)/shard_map/ppermute | solution.py:21
  468.5 78.7 %collective-permute-start.21 = (bf16[1,64,128]{2,0,1:T(2,128)(2,1)S(1)}, bf16[1,64,128]{2,0,1:T(2,128)(2,1)S(1)}, u32[]{:S(2)}, u32[]{:S(2)}) collective-permute-start(bf16[1,64,128]{2,0,1:T(2,128)(2,1)S(1)} %get-tuple-element.54), channel_id=1, source_target_pairs={{8,0},{16,8},{24,16},{32,24},{40,32},{48,40},{56,48},{64,56},{72,6... | collective-permute-start | bytes 49160 | tf_op jit(solution)/shard_map/ppermute | solution.py:22
  547.3 5.0 collective-permute-start.22
  555.8 5.3 collective-permute-start.24
  564.2 7.9 %collective-permute-start.26 = (bf16[18,1,128]{2,0,1:T(8,128)(2,1)S(1)}, bf16[18,1,128]{2,0,1:T(8,128)(2,1)S(1)}, u32[]{:S(2)}, u32[]{:S(2)}) collective-permute-start(bf16[18,1,128]{2,0,1:T(8,128)(2,1)S(1)} %get-tuple-element.43), channel_id=1, source_target_pairs={{0,1},{1,2},{2,3},{3,4},{4,5},{5,6},{6,7},{8,9},{9,10},{10,11},{11... | collective-permute-start | bytes 13832 | tf_op jit(solution)/shard_map/ppermute | solution.py:21
  578.3 5.1 collective-permute-start.29
  583.5 6.9 collective-permute-start.30
  603.3 5.0 collective-permute-start.33
  608.4 5.6 collective-permute-start.34
  643.4 5.0 collective-permute-start.36
  651.0 6.1 collective-permute-start.38
  654.3 5.2 collective-permute-start.39
  (46 other events, 1056.7 us)
Sparse Core Ops, SparseCore 0:
  219.7 242.5 all-reduce.3
where the time goes:
time: 762 us; the launch traced here: 757 us
  waiting for transfers between devices  293 us (38%)
  blocking collectives  239 us (31%)
  starting transfers between devices  97.2 us (13%)
  matrix products  63.9 us (8%)
  local copies, waits for them, and re-layouts  26.2 us (3%)
  other arithmetic  20.2 us (3%)
  between operations  18.2 us (2%)
    psum x1, waiting for transfers between devices, local(): total_low, total_high = lax.psum((part_low, part_high), ('row', 'col'))  242 us
    psum x1, blocking collectives, local(): lax.psum((jnp.sum(group_view, axis=(0, 2)), jnp.sum(group_view * group_vi...  81.4 us
    psum x1, blocking collectives, local(): lax.psum((jnp.sum(group_view_gradient, axis=(0, 2)), jnp.sum(group_view_g...  80.2 us
    psum x1, blocking collectives, local(): total_low, total_high = lax.psum((part_low, part_high), ('row', 'col'))  77.1 us
    ppermute x20, starting transfers between devices, extended(): before = lax.ppermute(last, axis, up)  62.8 us
    conv_general_dilated x10, matrix products, conv_valid(): lax.conv_general_dilated(padded[None], kernel, (1, 1), 'VALID', dimension...  61.7 us
    ppermute x20, waiting for transfers between devices, extended(): after = lax.ppermute(leading, axis, down)  50.2 us
    ppermute x20, starting transfers between devices, extended(): after = lax.ppermute(leading, axis, down)  34.4 us
  transfers between devices with their start and end apart: 41, of which 19 were waited for; matrix products, arithmetic and copies ran while one was open for 1% of the time, Pallas kernels for 0%

commit v1 on v0

v1 whole, which is shorter than its diff:
```python
import jax
import jax.numpy as jnp
from jax import lax
from jax.experimental import pallas as pl
from jax.experimental.pallas import tpu as pltpu
from jax.sharding import PartitionSpec as P

GROUPS = 32
EPS = 1e-05
PIX_MEAN = (0.485, 0.456, 0.406)
PIX_STD = (0.229, 0.224, 0.225)
HALO = 16
F32 = jnp.float32
BF16 = jnp.bfloat16
INTERPRET = False
HIGH = lax.Precision.HIGHEST


def padded_dy(w, before, after):
    return jnp.pad(w, ((before, after), (0, 0), (0, 0), (0, 0)))


def flipped(w):
    return jnp.transpose(w[::-1, ::-1], (0, 1, 3, 2))


def pack_stream(w, order):
    wz = padded_dy(w, 1, 1)
    both = jnp.stack([wz[1:5], wz[0:4]], axis=0)
    both = jnp.stack([both[:, j] for j in order], axis=0)
    cin, cout = w.shape[2], w.shape[3]
    return jnp.transpose(both, (0, 3, 2, 1, 4)).reshape(4 * cin, 6 * cout)


def pack_narrow_out(w):
    cin, cout = w.shape[2], w.shape[3]
    wz = jnp.pad(w, ((2, 2), (0, 0), (0, 0), (0, 4 - cout)))
    parts = [wz[i - q - 2 * s + 3] for s in (0, -1, 1) for q in (0, 1) for i in (0, 1)]
    v = jnp.stack(parts, 0).reshape(3, 2, 2, 3, cin, 4)
    return jnp.transpose(v, (0, 3, 1, 5, 2, 4)).reshape(72, 2 * cin)


def pack_narrow_in(w):
    cin, cout = w.shape[2], w.shape[3]
    wz = jnp.pad(w, ((2, 2), (0, 0), (0, 4 - cin), (0, 0)))
    parts = [wz[2 * s + i - q + 3] for s in (-1, 0, 1) for i in (0, 1) for q in (0, 1)]
    v = jnp.stack(parts, 0).reshape(3, 2, 2, 3, 4, cout)
    v = jnp.transpose(v, (0, 3, 1, 4, 2, 5)).reshape(3, 24, 2 * cout)
    return jnp.pad(v, ((0, 0), (0, 8), (0, 0))).reshape(96, 2 * cout)


def iota(shape, axis):
    return lax.broadcasted_iota(jnp.int32, shape, axis)


def group_rows(s, q, channels):
    per = channels // GROUPS
    c = iota((channels, 128), 0) // per
    l = iota((channels, 128), 1)
    g1 = jnp.where(l == c, 1.0, 0.0).astype(F32)
    g2 = jnp.where(l == c + GROUPS, 1.0, 0.0).astype(F32)
    out = jnp.dot(s, g1, precision=HIGH, preferred_element_type=F32)
    out = out + jnp.dot(q, g2, precision=HIGH, preferred_element_type=F32)
    return jnp.sum(out, axis=0, keepdims=True)


def group_values(rows, channels, count):
    per = channels // GROUPS
    tot = jnp.sum(rows, axis=0, keepdims=True) * (1.0 / count)
    tot = jnp.broadcast_to(tot, (8, 128))
    l = iota((128, channels), 0)
    c = iota((128, channels), 1) // per
    e1 = jnp.where(l == c, 1.0, 0.0).astype(F32)
    e2 = jnp.where(l == c + GROUPS, 1.0, 0.0).astype(F32)
    a = jnp.dot(tot, e1, precision=HIGH, preferred_element_type=F32)[0:1]
    b = jnp.dot(tot, e2, precision=HIGH, preferred_element_type=F32)[0:1]
    return a, b


def norm_values(rows, channels, count):
    mean, msq = group_values(rows, channels, count)
    return mean, lax.rsqrt(msq - mean * mean + EPS)


def gelu_both(a):
    e = jnp.exp(a * a * -0.5)
    t = 1.0 / (1.0 + jnp.abs(a) * (0.3275911 * 0.7071067811865476))
    poly = t * (
        0.5 * 0.254829592
        + t
        * (0.5 * -0.284496736 + t * (0.5 * 1.421413741 + t * (0.5 * -1.453152027 + t * (0.5 * 1.061405429))))
    )
    q = poly * e
    phi = jnp.where(a >= 0.0, 1.0 - q, q)
    return a * phi, phi + a * e * 0.3989422804014327


def taps(p, n):
    m = p.shape[0]
    return pltpu.roll(p[:, 0:n], 1, 0) + p[:, n : 2 * n] + pltpu.roll(p[:, 2 * n : 3 * n], m - 1, 0)


def lane_taps(c):
    return pltpu.roll(c[0:8], 1, 1) + c[8:16] + pltpu.roll(c[16:24], 255, 1)


def nt(a, b):
    return lax.dot_general(a, b, (((1,), (1,)), ((), ())), preferred_element_type=F32)


def tn(a, b):
    return lax.dot_general(a, b, (((0,), (0,)), ((), ())), preferred_element_type=F32)


def loop(lo, hi, body):
    lax.fori_loop(lo, hi, lambda i, c: (body(i), c)[1], 0)


def color_column(values):
    c = iota((8, 1), 0) % 4
    out = jnp.zeros((8, 1), F32)
    for k, v in enumerate(values):
        out = jnp.where(c == k, v, out)
    return out


def stats_kernel(n, x_ref, o_ref):
    rows, cols, channels = x_ref.shape

    def body(r, carry):
        s, q = carry
        x = x_ref[r].astype(F32).reshape(cols // 8, 8, channels)
        return s + jnp.sum(x, axis=0), q + jnp.sum(x * x, axis=0)

    z = jnp.zeros((8, channels), F32)
    s, q = lax.fori_loop(0, rows, body, (z, z))
    o_ref[...] = jnp.broadcast_to(group_rows(s, q, channels), (n, 128))


def forward_kernel(
    dims,
    idx,
    dbias,
    lat_hbm,
    up,
    down,
    left,
    right,
    ul,
    ur,
    dl,
    dr,
    stats,
    vecs,
    wd,
    w1,
    w2,
    w3,
    w4,
    gram,
    slope1,
    feat2,
    slope2,
    slope3,
    feat4,
    slope4,
    sact,
    lat,
    tt,
    pixcol,
    y1,
    f2,
    yp,
    f3,
    fm,
    sems,
):
    rows, cols, image_rows, image_cols, count = dims
    h = HALO
    width = cols + 2 * h
    half = width // 2
    pairs = (rows + 2 * h) // 2
    pieces = (
        (lat_hbm, lat.at[pl.ds(h, rows), pl.ds(h, cols)]),
        (up, lat.at[pl.ds(0, h), pl.ds(h, cols)]),
        (down, lat.at[pl.ds(h + rows, h), pl.ds(h, cols)]),
        (left, lat.at[pl.ds(h, rows), pl.ds(0, h)]),
        (right, lat.at[pl.ds(h, rows), pl.ds(h + cols, h)]),
        (ul, lat.at[pl.ds(0, h), pl.ds(0, h)]),
        (ur, lat.at[pl.ds(0, h), pl.ds(h + cols, h)]),
        (dl, lat.at[pl.ds(h + rows, h), pl.ds(0, h)]),
        (dr, lat.at[pl.ds(h + rows, h), pl.ds(h + cols, h)]),
    )
    copies = [pltpu.make_async_copy(a, b, sems.at[i]) for i, (a, b) in enumerate(pieces)]
    for c in copies:
        c.start()

    tt[:, :, 128:256] = jnp.zeros((pairs, 72, 128), F32)
    pixcol[...] = jnp.zeros(pixcol.shape, BF16)
    yp[...] = jnp.zeros(yp.shape, BF16)

    row0 = idx[0] * rows - h
    col0 = idx[1] * cols - h

    def valid_rows(r):
        return jnp.where((row0 + r >= 0) & (row0 + r < image_rows), 1.0, 0.0).astype(F32)

    def col_mask(n, step, lanes):
        c = col0 + step * iota((n, lanes), 0)
        return jnp.where((c >= 0) & (c < image_cols), 1.0, 0.0).astype(F32)

    cmask = col_mask(width, 1, 128)
    hmask = col_mask(half, 2, 128)
    lane = iota((8, 256), 1)
    lmask = jnp.where((col0 + lane >= 0) & (col0 + lane < image_cols) & (lane < width), 1.0, 0.0)
    lmask = lmask.astype(F32)

    mean, rstd = norm_values(stats[...], 128, count)
    gain = vecs[0:1]
    scale = rstd * gain
    shift = vecs[1:2] - mean * scale
    b1, b2, b3, b4 = vecs[2:3], vecs[3:4], vecs[4:5], vecs[5:6]

    for c in copies:
        c.wait()

    def act_row(r):
        t = lat[r].astype(F32) * scale + shift
        sig = 0.5 * jnp.tanh(0.5 * t) + 0.5
        return t, sig

    def decode(p):
        parts = []
        m = cmask * valid_rows(2 * p)
        for i in range(2):
            t, sig = act_row(2 * p + i)
            parts.append((t * sig * m).astype(BF16))
        tt[p, :, 0:width] = nt(wd[...], jnp.concatenate(parts, axis=1))

    loop(0, pairs, decode)

    def slopes(r):
        t = lat[r + h, pl.ds(h, cols), :].astype(F32) * scale + shift
        sig = 0.5 * jnp.tanh(0.5 * t) + 0.5
        sact[r] = (sig * (1.0 + t * (1.0 - sig)) * gain).astype(BF16)

    loop(0, rows, slopes)

    pscale = color_column([0.5 / s for s in PIX_STD])
    pbias = color_column([((dbias[k] + 1.0) * 0.5 - PIX_MEAN[k]) * (1.0 / PIX_STD[k]) for k in range(3)])

    def pixels(p):
        c = tt[p, 0:24] + tt[p + 1, 24:48] + tt[p - 1, 48:72]
        x = (lane_taps(c) * pscale + pbias) * (lmask * valid_rows(2 * p))
        z = jnp.zeros((8, 256), F32)
        pixcol[p] = jnp.concatenate([pltpu.roll(x, 1, 1), x, pltpu.roll(x, 255, 1), z], axis=0).astype(BF16)

    loop(1, pairs - 1, pixels)

    def first(p):
        lhs = pixcol[pl.ds(p - 1, 3), :, 0:width].reshape(96, width)
        g, s = gelu_both(tn(lhs, w1[...]) + b1)
        m = cmask * valid_rows(2 * p)
        f = (g * m).astype(BF16)
        y1[p, :, 0:128] = f
        y1[p - 1, :, 128:192] = f[:, 0:64]
        y1[p + 1, :, 192:256] = f[:, 64:128]

        @pl.when((p >= 7) & (p < 25))
        def _():
            slope1[p - 7] = (s * m).astype(BF16)

    loop(1, pairs - 1, first)

    pr = iota((half, width), 0)
    pc = iota((half, width), 1) // 2
    pool = jnp.where(pr == pc, 0.25, 0.0).astype(BF16)

    def second(g):
        p0 = 2 + 4 * g
        x = y1[pl.ds(p0, 4)].reshape(4 * width, 256)
        pre = taps(jnp.dot(x, w2[...], preferred_element_type=F32), 128) + b2
        f, s = gelu_both(pre)
        for i in range(4):
            p = p0 + i
            m = cmask * valid_rows(2 * p)
            fi = (f[i * width : (i + 1) * width] * m).astype(BF16)
            f2[p] = fi
            half_sum = jnp.dot(pool, fi, preferred_element_type=F32)
            v = (half_sum + pltpu.roll(half_sum, 64, 1)).astype(BF16)
            k = 1 + 2 * g + i // 2
            if i % 2 == 0:
                yp[k, :, 0:64] = v[:, 0:64]
                yp[k - 1, :, 128:192] = v[:, 0:64]
            else:
                yp[k, :, 64:128] = v[:, 64:128]
                yp[k + 1, :, 192:256] = v[:, 64:128]

            @pl.when((p >= 6) & (p < 26))
            def _():
                feat2[p - 6] = fi
                slope2[p - 6] = (s[i * width : (i + 1) * width] * m).astype(BF16)

    loop(0, 7, second)

    def wide(g, w, src, stacked):
        k0 = stacked + 2 * g
        lhs = []
        for i in range(2):
            r = 2 * (k0 + i)
            lhs.append(jnp.concatenate([src[r - 1], src[r], src[r + 1], src[r + 2]], axis=1))
        return taps(jnp.dot(jnp.concatenate(lhs, axis=0), w[...], preferred_element_type=F32), 256)

    b33 = jnp.concatenate([b3, b3], axis=1)
    b44 = jnp.concatenate([b4, b4], axis=1)

    def third(g):
        k0 = 1 + 2 * g
        x = yp[pl.ds(k0, 2)].reshape(2 * half, 256)
        f, s = gelu_both(taps(jnp.dot(x, w3[...], preferred_element_type=F32), 256) + b33)
        for i in range(2):
            m = hmask * valid_rows(4 * (k0 + i))
            for q in range(2):
                r = 2 * (k0 + i) + q
                at = (slice(i * half, (i + 1) * half), slice(q * 128, (q + 1) * 128))
                f3[r] = (f[at] * m).astype(BF16)
                slope3[r] = (s[at] * m).astype(BF16)

    loop(0, 7, third)

    own = iota((half, 128), 0)
    omask = jnp.where((own >= h // 2) & (own < h // 2 + cols // 2), 1.0, 0.0).astype(F32)

    def fourth(g):
        k0 = 2 + 2 * g
        f, s = gelu_both(wide(g, w4, f3, 2) + b44)
        for i in range(2):
            m = hmask * valid_rows(4 * (k0 + i))
            for q in range(2):
                r = 2 * (k0 + i) + q
                at = (slice(i * half, (i + 1) * half), slice(q * 128, (q + 1) * 128))
                feat4[r - 4] = (f[at] * m).astype(BF16)
                slope4[r - 4] = (s[at] * m).astype(BF16)

                @pl.when((r >= 8) & (r < 24))
                def _():
                    fm[r - 8] = (f[at] * omask).astype(BF16)

    loop(0, 6, fourth)

    a = fm[...].reshape(16 * half, 128)
    gram[0:128] = tn(a, a)
    b = f2[8:24, h : h + cols, :].reshape(16 * cols, 128)
    gram[128:256] = tn(b, b)


def backward_kernel(
    dims,
    idx,
    totals,
    exlow,
    exhigh,
    slope1,
    feat2,
    slope2,
    slope3,
    feat4,
    slope4,
    sact,
    lat,
    stats,
    w4t,
    w3t,
    w2t,
    w1t,
    wdt,
    dxh,
    sums,
    loss,
    sw1,
    sw2,
    b4,
    b3,
    y2,
    tt,
    brgb,
):
    rows, cols, image_rows, image_cols, count = dims
    h = HALO
    width = cols + 2 * h
    half = width // 2
    npix = image_rows * image_cols
    row0 = idx[0] * rows - h
    col0 = idx[1] * cols - h

    def valid_rows(r):
        return jnp.where((row0 + r >= 0) & (row0 + r < image_rows), 1.0, 0.0).astype(F32)

    lane = iota((8, 256), 1)
    lmask = jnp.where((col0 + lane >= 0) & (col0 + lane < image_cols) & (lane < width), 1.0, 0.0)
    lmask = lmask.astype(F32)

    g1 = totals[128:256]
    g1 = g1 + pltpu.roll(pltpu.roll(g1, 64, 0), 64, 1)
    same = (iota((128, 128), 0) // 64) == (iota((128, 128), 1) // 64)
    gap1 = jnp.where(same, g1 * (1.0 / npix) - exlow[...], 0.0)
    gap2 = totals[0:128] * (4.0 / npix) - exhigh[...]
    value = jnp.sum(gap1 * gap1) * (0.5 / 4096.0) + jnp.sum(gap2 * gap2) * (1.0 / 16384.0)
    loss[...] = jnp.broadcast_to(value, loss.shape)
    for gap, sw in ((gap1, sw1), (gap2, sw2)):
        sym = 2.0 * (gap + gap.T)
        upper = sym.astype(BF16)
        sw[0:128] = upper
        sw[128:256] = (sym - upper.astype(F32)).astype(BF16)

    zrow = jnp.zeros((half, 128), BF16)
    b4[3] = zrow
    b4[28] = zrow
    tt[6] = jnp.zeros((72, 256), F32)
    tt[25] = jnp.zeros((72, 256), F32)
    tt[:, :, 128:256] = jnp.zeros((tt.shape[0], 72, 128), F32)

    def back4(g):
        x = feat4[pl.ds(4 * g, 4)].reshape(4 * half, 128)
        y = jnp.dot(jnp.concatenate([x, x], axis=1), sw2[...], preferred_element_type=F32)
        y = y * slope4[pl.ds(4 * g, 4)].reshape(4 * half, 128).astype(F32)
        b4[pl.ds(4 + 4 * g, 4)] = y.astype(BF16).reshape(4, half, 128)

    loop(0, 6, back4)

    def wide(k0, w, src, n):
        lhs = []
        for i in range(2):
            r = 2 * (k0 + i)
            lhs.append(jnp.concatenate([src[r - 1], src[r], src[r + 1], src[r + 2]], axis=1))
        return taps(jnp.dot(jnp.concatenate(lhs, axis=0), w[...], preferred_element_type=F32), n)

    def back3(g):
        k0 = 2 + 2 * g
        y = wide(k0, w4t, b4, 256)
        for i in range(2):
            for q in range(2):
                r = 2 * (k0 + i) + q
                part = y[i * half : (i + 1) * half, q * 128 : (q + 1) * 128]
                b3[r] = (part * slope3[r].astype(F32)).astype(BF16)

    loop(0, 6, back3)

    ur = iota((width, width), 0) // 2
    uc = iota((width, width), 1) % half
    spread = jnp.where(ur == uc, 0.25, 0.0).astype(BF16)
    first_half = iota((width, 128), 1) < 64

    def back2(g):
        k0 = 3 + 2 * g
        y = wide(k0, w3t, b3, 128)
        for i in range(2):
            gp = y[i * half : (i + 1) * half]
            upper = gp.astype(BF16)
            lower = (gp - upper.astype(F32)).astype(BF16)
            r = jnp.dot(spread, jnp.concatenate([upper, lower], axis=0), preferred_element_type=F32)
            rr = pltpu.roll(r, 64, 1)
            for q in range(2):
                p = 2 * (k0 + i) + q
                sp = jnp.where(first_half, r, rr) if q == 0 else jnp.where(first_half, rr, r)
                x = feat2[p - 6]
                gt = jnp.dot(jnp.concatenate([x, x], axis=1), sw1[...], preferred_element_type=F32)
                b = ((sp + gt) * slope2[p - 6].astype(F32)).astype(BF16)
                y2[p, :, 0:128] = b
                y2[p - 1, :, 128:192] = b[:, 0:64]
                y2[p + 1, :, 192:256] = b[:, 64:128]

    loop(0, 5, back2)

    def back1(g):
        p0 = 7 + 3 * g
        x = y2[pl.ds(p0, 3)].reshape(3 * width, 256)
        y = taps(jnp.dot(x, w2t[...], preferred_element_type=F32), 128)
        for i in range(3):
            b = (y[i * width : (i + 1) * width] * slope1[p0 + i - 7].astype(F32)).astype(BF16)
            tt[p0 + i, :, 0:width] = nt(w1t[...], b)

    loop(0, 6, back1)

    pscale = color_column([0.5 / s for s in PIX_STD])

    def colors(p):
        c = tt[p, 0:24] + tt[p + 1, 24:48] + tt[p - 1, 48:72]
        x = lane_taps(c) * pscale * (lmask * valid_rows(2 * p))
        parts = [pltpu.roll(x, 256 - h + d, 1)[:, 0:cols] for d in (1, 0, -1)]
        z = jnp.zeros((8, cols), F32)
        brgb[p] = jnp.concatenate(parts + [z], axis=0).astype(BF16)

    loop(7, 25, colors)

    mean, rstd = norm_values(stats[...], 128, count)
    offset = mean * rstd

    def last(p, carry):
        s, q = carry
        y = tn(brgb[pl.ds(p - 1, 3)].reshape(96, cols), wdt[...])
        for i in range(2):
            r = 2 * (p - 8) + i
            d = y[:, i * 128 : (i + 1) * 128] * sact[r].astype(F32)
            xh = lat[r].astype(F32) * rstd - offset
            dxh[r] = d.astype(BF16)
            s = s + jnp.sum(d.reshape(cols // 8, 8, 128), axis=0)
            q = q + jnp.sum((d * xh).reshape(cols // 8, 8, 128), axis=0)
        return s, q

    z = jnp.zeros((8, 128), F32)
    s, q = lax.fori_loop(8, 24, last, (z, z))
    sums[...] = jnp.broadcast_to(group_rows(s, q, 128), sums.shape)


def final_kernel(count, lat, dxh, stats, sums, out):
    mean, rstd = norm_values(stats[...], 128, count)
    n1, n2 = group_values(sums[...], 128, count)
    b = rstd * rstd * n2
    c = rstd * n1 - b * mean
    for r in range(out.shape[0]):
        y = dxh[r].astype(F32) * rstd - lat[r].astype(F32) * b - c
        out[r] = y.astype(BF16)


def full(shape):
    return pl.BlockSpec(shape, lambda *_: (0,) * len(shape))


def call(kernel, outs, scratch, args, kinds):
    specs = []
    for a, k in zip(args, kinds):
        if k == "s":
            specs.append(pl.BlockSpec(memory_space=pltpu.SMEM))
        elif k == "a":
            specs.append(pl.BlockSpec(memory_space=pl.ANY))
        else:
            specs.append(pl.BlockSpec(memory_space=pltpu.VMEM))
    return pl.pallas_call(
        kernel,
        out_shape=[jax.ShapeDtypeStruct(s, d) for s, d in outs],
        in_specs=specs,
        out_specs=[pl.BlockSpec(memory_space=pltpu.VMEM) for _ in outs],
        scratch_shapes=scratch,
        compiler_params=pltpu.CompilerParams(vmem_limit_bytes=56 * 1024 * 1024),
        interpret=INTERPRET,
    )(*args)


def local(
    latent,
    gain,
    bias,
    decoder_weight,
    decoder_bias,
    first_weight,
    first_bias,
    second_weight,
    second_bias,
    third_weight,
    third_bias,
    fourth_weight,
    fourth_bias,
    exemplar_low,
    exemplar_high,
):
    rows, cols, channels = latent.shape
    nrow, ncol = lax.axis_size("row"), lax.axis_size("col")
    n = nrow * ncol
    both = ("row", "col")
    h = HALO
    width = cols + 2 * h
    half = width // 2
    pairs = (rows + 2 * h) // 2
    image_rows, image_cols = rows * nrow, cols * ncol
    count = image_rows * image_cols * (channels // GROUPS)
    dims = (rows, cols, image_rows, image_cols, count)

    def shifted(x, dr, dc):
        perm = []
        for r in range(nrow):
            for c in range(ncol):
                a, b = r + dr, c + dc
                if 0 <= a < nrow and 0 <= b < ncol:
                    perm.append((r * ncol + c, a * ncol + b))
        return lax.ppermute(x, both, perm)

    up = shifted(latent[rows - h :], 1, 0)
    down = shifted(latent[:h], -1, 0)
    left = shifted(latent[:, cols - h :], 0, 1)
    right = shifted(latent[:, :h], 0, -1)
    ul = shifted(latent[rows - h :, cols - h :], 1, 1)
    ur = shifted(latent[rows - h :, :h], 1, -1)
    dl = shifted(latent[:h, cols - h :], -1, 1)
    dr = shifted(latent[:h, :h], -1, -1)

    def everyone(x):
        return lax.all_to_all(x, both, 0, 0, tiled=True)

    (mine,) = call(lambda *r: stats_kernel(n, *r), [((n, 128), F32)], [], [latent], "v")
    stats = everyone(mine)

    idx = jnp.stack([lax.axis_index("row"), lax.axis_index("col")]).astype(jnp.int32)
    vecs = jnp.concatenate(
        [
            gain,
            bias,
            first_bias,
            first_bias,
            second_bias,
            second_bias,
            third_bias,
            fourth_bias,
            jnp.zeros((256,), F32),
        ]
    ).reshape(8, 128)
    packed_order = (1, 2, 3, 0)
    row_order = (0, 1, 2, 3)
    wd = pack_narrow_out(decoder_weight)
    w1 = pack_narrow_in(first_weight)
    w2 = pack_stream(second_weight, packed_order)
    w3 = pack_stream(third_weight, packed_order)
    w4 = pack_stream(fourth_weight, row_order)
    w4t = pack_stream(flipped(fourth_weight), row_order)
    w3t = pack_stream(flipped(third_weight), row_order)
    w2t = pack_stream(flipped(second_weight), packed_order)
    w1t = pack_narrow_out(flipped(first_weight))
    wdt = pack_narrow_in(flipped(decoder_weight))

    states = call(
        lambda *r: forward_kernel(dims, *r),
        [
            ((256, 128), F32),
            ((18, width, 128), BF16),
            ((20, width, 128), BF16),
            ((20, width, 128), BF16),
            ((32, half, 128), BF16),
            ((24, half, 128), BF16),
            ((24, half, 128), BF16),
            ((rows, cols, 128), BF16),
        ],
        [
            pltpu.VMEM((2 * pairs, width, 128), BF16),
            pltpu.VMEM((pairs, 72, 256), F32),
            pltpu.VMEM((pairs, 32, 256), BF16),
            pltpu.VMEM((pairs, width, 256), BF16),
            pltpu.VMEM((pairs, width, 128), BF16),
            pltpu.VMEM((pairs // 2, half, 256), BF16),
            pltpu.VMEM((pairs, half, 128), BF16),
            pltpu.VMEM((16, half, 128), BF16),
            pltpu.SemaphoreType.DMA((9,)),
        ],
        [idx, decoder_bias, latent, up, down, left, right, ul, ur, dl, dr, stats, vecs, wd, w1, w2, w3, w4],
        "ss" + "a" * 9 + "v" * 7,
    )
    gram = states[0]
    mine = everyone(gram).reshape(n, 256 // n, 128).sum(axis=0)
    totals = everyone(jnp.broadcast_to(mine[None], (n, 256 // n, 128)).reshape(256, 128))
    exlow = jnp.tile(exemplar_low, (2, 2))

    dxh, sums, loss = call(
        lambda *r: backward_kernel(dims, *r),
        [((rows, cols, 128), BF16), ((n, 128), F32), ((8, 128), F32)],
        [
            pltpu.VMEM((256, 128), BF16),
            pltpu.VMEM((256, 128), BF16),
            pltpu.VMEM((pairs, half, 128), BF16),
            pltpu.VMEM((pairs, half, 128), BF16),
            pltpu.VMEM((pairs, width, 256), BF16),
            pltpu.VMEM((pairs, 72, 256), F32),
            pltpu.VMEM((pairs, 32, cols), BF16),
        ],
        [idx, totals, exlow, exemplar_high, *states[1:], latent, stats, w4t, w3t, w2t, w1t, wdt],
        "s" + "v" * 17,
    )
    sums = everyone(sums)

    step = 8
    blk = pl.BlockSpec((step, cols, 128), lambda i: (i, 0, 0))
    out = pl.pallas_call(
        lambda *r: final_kernel(count, *r),
        out_shape=jax.ShapeDtypeStruct((rows, cols, channels), BF16),
        grid=(rows // step,),
        in_specs=[blk, blk, full((n, 128)), full((n, 128))],
        out_specs=blk,
        interpret=INTERPRET,
    )(latent, dxh, stats, sums)
    return out, loss[0, 0]


def solution(mesh):
    placed = (P("row", "col", None),) + (P(),) * 14
    return jax.shard_map(
        local, mesh=mesh, in_specs=placed, out_specs=(P("row", "col", None), P()), check_vma=False
    )
```

time: 762 us -> 211 us (0.28)
  waiting for transfers between devices: 293 us -> 34 us
  blocking collectives: 239 us -> 0 us
  Pallas kernels: 0 us -> 68.1 us
  matrix products: 63.9 us -> 0 us
  starting transfers between devices: 97.2 us -> 68.8 us
  other arithmetic: 20.2 us -> 2.55 us
  between operations: 18.2 us -> 1.36 us
  local copies, waits for them, and re-layouts: 26.2 us -> 35 us
    psum x1 -> x0, waiting for transfers between devices: 242 us -> none  [local(): total_low, total_high = lax.psum((part_low, part_high), ('row', 'col'))]
    psum x3 -> x0, blocking collectives: 239 us -> none  [the longest x1 81.4 us: local(): lax.psum((jnp.sum(group_view, axis=(0, 2)), jnp.sum(group_view * group_vi...]
    ppermute x40 -> x8, starting transfers between devices: 97.1 us -> 21.8 us  [shifted(): return lax.ppermute(x, both, perm)]
    pallas_call x0 -> x4, Pallas kernels: none -> 68.1 us  [the longest x3 63.7 us: call(): pl.pallas_call(kernel, out_shape=[jax.ShapeDtypeStruct(s, d) for s, d in...]
    conv_general_dilated x10 -> x0, matrix products: 61.7 us -> none  [conv_valid(): lax.conv_general_dilated(padded[None], kernel, (1, 1), 'VALID', dimension...]
    all_to_all x0 -> x4, starting transfers between devices: none -> 47 us  [everyone(): return lax.all_to_all(x, both, 0, 0, tiled=True)]
    ppermute x40 -> x8, waiting for transfers between devices: 50.3 us -> 5.79 us  [shifted(): return lax.ppermute(x, both, perm)]
    all_to_all x0 -> x4, waiting for transfers between devices: none -> 28.2 us  [everyone(): return lax.all_to_all(x, both, 0, 0, tiled=True)]
  transfers between devices with their start and end apart: 41 -> 12, of which waited for: 19 -> 4; matrix products, arithmetic and copies ran while one was open for 1% -> 13% of each run, Pallas kernels for 0% -> 1%
where the time goes in v1:
time: 211 us; the launch traced here: 210 us
  starting transfers between devices  68.8 us (33%)
  Pallas kernels  68.1 us (32%)
  local copies, waits for them, and re-layouts  35 us (17%)
  waiting for transfers between devices  34 us (16%)
  other arithmetic  2.55 us (1%)
    pallas_call x3, Pallas kernels, call(): pl.pallas_call(kernel, out_shape=[jax.ShapeDtypeStruct(s, d) for s, d in...  63.7 us
    all_to_all x4, starting transfers between devices, everyone(): return lax.all_to_all(x, both, 0, 0, tiled=True)  47 us
    all_to_all x4, waiting for transfers between devices, everyone(): return lax.all_to_all(x, both, 0, 0, tiled=True)  28.2 us
    ppermute x8, starting transfers between devices, shifted(): return lax.ppermute(x, both, perm)  21.8 us
    unnamed x99, local copies, waits for them, and re-layouts  13.9 us
    reshape x7, local copies, waits for them, and re-layouts, pack_stream(): return jnp.transpose(both, (0, 3, 2, 1, 4)).reshape(4 * cin, 6 * cout)  7.67 us
    ppermute x8, waiting for transfers between devices, shifted(): return lax.ppermute(x, both, perm)  5.79 us
    pallas_call x1, Pallas kernels, local(): pl.pallas_call(lambda *r: final_kernel(count, *r), out_shape=jax.ShapeDty...  4.45 us
  transfers between devices with their start and end apart: 12, of which 4 were waited for; matrix products, arithmetic and copies ran while one was open for 13% of the time, Pallas kernels for 1%

profile of v1, /device:TPU:1, one launch (start us, length us, event | category | flops | bytes accessed | tf_op | source)
XLA Modules:
  0.0 209.9 jit_solution(8779316080898001950)
XLA Ops:
  0.6 1.7 fusion.54
  2.4 5.9 %collective-permute-start.4 = (bf16[16,16,128]{2,1,0:T(8,128)(2,1)}, bf16[16,16,128]{2,1,0:T(8,128)(2,1)S(1)}, u32[]{:S(2)}, u32[]{:S(2)}) collective-permute-start(bf16[16,16,128]{2,1,0:T(8,128)(2,1)} %get-tuple-element.27), channel_id=1, source_target_pairs={{0,9},{1,10},{2,11},{3,12},{4,13},{5,14},{6,15},{8,17},{9,18},{10,... | collective-permute-start | bytes 196616 | tf_op jit(solution)/shard_map/ppermute | solution.py:586
  8.3 2.3 %collective-permute-start.5 = (bf16[16,16,128]{2,1,0:T(8,128)(2,1)}, bf16[16,16,128]{2,1,0:T(8,128)(2,1)S(1)}, u32[]{:S(2)}, u32[]{:S(2)}) collective-permute-start(bf16[16,16,128]{2,1,0:T(8,128)(2,1)} %get-tuple-element.26), channel_id=1, source_target_pairs={{1,8},{2,9},{3,10},{4,11},{5,12},{6,13},{7,14},{9,16},{10,17},{11,... | collective-permute-start | bytes 196616 | tf_op jit(solution)/shard_map/ppermute | solution.py:586
  10.6 1.3 collective-permute-start.6
  11.9 2.8 %shard_map.158 = f32[256,128]{1,0:T(8,128)} custom-call(bf16[32,128,128]{2,1,0:T(8,128)(2,1)} %r_0_.3), custom_call_target="tpu_custom_call" | custom-call | tf_op jit(solution)/shard_map/pallas_call | solution.py:539
  14.7 17.2 %all-to-all-start = ((f32[256,1,128]{2,1,0:T(1,128)}), f32[256,1,128]{2,1,0:T(1,128)S(1)}, u32[]{:S(2)}, u32[]{:S(2)}) async-start(f32[256,1,128]{2,1,0:T(1,128)} %bitcast.169), calls=%async_computation | async-start | bytes 262144 | tf_op jit(solution)/shard_map/all_to_all | solution.py:598
  33.0 4.2 %collective-permute-start = (bf16[16,128,128]{2,1,0:T(8,128)(2,1)}, bf16[16,128,128]{2,1,0:T(8,128)(2,1)}, u32[]{:S(2)}, u32[]{:S(2)}) collective-permute-start(bf16[16,128,128]{2,1,0:T(8,128)(2,1)} %get-tuple-element.31), channel_id=1, source_target_pairs={{0,8},{1,9},{2,10},{3,11},{4,12},{5,13},{6,14},{7,15},{8,16},{9,17... | collective-permute-start | bytes 1572872 | tf_op jit(solution)/shard_map/ppermute | solution.py:586
  37.2 1.3 collective-permute-start.1
  50.7 3.7 %collective-permute-start.2 = (bf16[32,16,128]{2,1,0:T(8,128)(2,1)S(1)}, bf16[32,16,128]{2,1,0:T(8,128)(2,1)S(1)}, u32[]{:S(2)}, u32[]{:S(2)}) collective-permute-start(bf16[32,16,128]{2,1,0:T(8,128)(2,1)S(1)} %get-tuple-element.29), channel_id=1, source_target_pairs={{0,1},{1,2},{2,3},{3,4},{4,5},{5,6},{6,7},{8,9},{9,10},{10,11},{11... | collective-permute-start | bytes 393224 | tf_op jit(solution)/shard_map/ppermute | solution.py:586
  54.5 1.9 collective-permute-start.3
  57.9 1.2 reshape.84.r_17_
  65.3 1.3 collective-permute-start.7
  67.2 5.8 %collective-permute-done.7.r_10_ = bf16[16,16,128]{2,1,0:T(8,128)(2,1)S(1)} collective-permute-done((bf16[16,16,128]{2,1,0:T(8,128)(2,1)S(1)}, bf16[16,16,128]{2,1,0:T(8,128)(2,1)S(1)}, u32[]{:S(2)}, u32[]{:S(2)}) %collective-permute-start.7) | collective-permute-done | bytes 65568 | tf_op jit(solution)/shard_map/ppermute | solution.py:586
  73.7 41.1 %shard_map.159 = (f32[256,128]{1,0:T(8,128)}, bf16[18,160,128]{2,1,0:T(8,128)(2,1)}, bf16[20,160,128]{2,1,0:T(8,128)(2,1)}, bf16[20,160,128]{2,1,0:T(8,128)(2,1)...) custom-call(s32[2]{0:T(128)} %pad_add_fusion.r_0_, ...), custom_call_target="tpu_custom_call" | custom-call | tf_op jit(solution)/shard_map/pallas_call | solution.py:539
  114.9 14.0 %all-to-all-start.1 = ((f32[256,1,128]{2,1,0:T(1,128)}), f32[256,1,128]{2,1,0:T(1,128)S(1)}, u32[]{:S(2)}, u32[]{:S(2)}) async-start(f32[256,1,128]{2,1,0:T(1,128)} %bitcast.175), calls=%async_computation.1 | async-start | bytes 262144 | tf_op jit(solution)/shard_map/all_to_all | solution.py:598
  129.1 12.7 %all-to-all-done.1 = f32[256,1,128]{2,1,0:T(1,128)S(1)} async-done(((f32[256,1,128]{2,1,0:T(1,128)}), f32[256,1,128]{2,1,0:T(1,128)S(1)}, u32[]{:S(2)}, u32[]{:S(2)}) %all-to-all-start.1) | async-done | bytes 131104 | tf_op jit(solution)/shard_map/all_to_all | solution.py:598
  142.7 5.9 %all-to-all-start.2 = ((f32[256,1,128]{2,1,0:T(1,128)}), f32[256,1,128]{2,1,0:T(1,128)S(1)}, u32[]{:S(2)}, u32[]{:S(2)}) async-start(f32[256,1,128]{2,1,0:T(1,128)} %reshape.85), calls=%async_computation.2 | async-start | bytes 262144 | tf_op jit(solution)/shard_map/all_to_all | solution.py:598
  151.2 1.2 reshape.86.r_13_
  153.5 1.3 reshape.94.r_14_
  157.7 3.9 %all-to-all-done.2 = f32[256,1,128]{2,1,0:T(1,128)S(1)} async-done(((f32[256,1,128]{2,1,0:T(1,128)}), f32[256,1,128]{2,1,0:T(1,128)S(1)}, u32[]{:S(2)}, u32[]{:S(2)}) %all-to-all-start.2) | async-done | bytes 131104 | tf_op jit(solution)/shard_map/all_to_all | solution.py:598
  162.2 19.8 %shard_map.160 = (bf16[32,128,128]{2,1,0:T(8,128)(2,1)}, f32[256,128]{1,0:T(8,128)}, f32[8,128]{1,0:T(8,128)}) custom-call(s32[2]{0:T(128)} %pad_add_fusion.r_0_, f32[256,128]{1,0:T(8,128)} %bitcast.168, f32[128,128]{1,0:T(8,128)} %tile.10.r_2_, f32[128,128]{1,0:T(8,128)} %r_3_.1, bf16[18,160,128]{2,1,0:T(8,128)(2,1)} %get-tuple-element.14.r_4_, ...), custom_call_target="tpu_custom_call" | custom-call | tf_op jit(solution)/shard_map/pallas_call | solution.py:539
  182.0 10.0 %all-to-all-start.3 = ((f32[256,1,128]{2,1,0:T(1,128)}), f32[256,1,128]{2,1,0:T(1,128)S(1)}, u32[]{:S(2)}, u32[]{:S(2)}) async-start(f32[256,1,128]{2,1,0:T(1,128)} %bitcast.176), calls=%async_computation.3 | async-start | bytes 262144 | tf_op jit(solution)/shard_map/all_to_all | solution.py:598
  193.2 11.6 %all-to-all-done.3 = f32[256,1,128]{2,1,0:T(1,128)S(1)} async-done(((f32[256,1,128]{2,1,0:T(1,128)}), f32[256,1,128]{2,1,0:T(1,128)S(1)}, u32[]{:S(2)}, u32[]{:S(2)}) %all-to-all-start.3) | async-done | bytes 131104 | tf_op jit(solution)/shard_map/all_to_all | solution.py:598
  205.5 4.5 %shard_map.161 = bf16[32,128,128]{2,1,0:T(8,128)(2,1)} custom-call(bf16[32,128,128]{2,1,0:T(8,128)(2,1)} %r_0_.3, bf16[32,128,128]{2,1,0:T(8,128)(2,1)} %get-tuple-element.21.r_1_, f32[256,128]{1,0:T(8,128)} %bitcast.167, f32[256,128]{1,0:T(8,128)} %bitcast.170), custom_call_target="tpu_custom_call" | custom-call | tf_op jit(solution)/shard_map/pallas_call | solution.py:680
  (162 shorter events, 32.1 us)
Async XLA Ops:
  0.6 31.3 %copy-start = (bf16[32,128,128]{2,1,0:T(8,128)(2,1)S(1)}, bf16[32,128,128]{2,1,0:T(8,128)(2,1)}, u32[]{:S(2)}) copy-start(bf16[32,128,128]{2,1,0:T(8,128)(2,1)} %r_0_.3) | copy-start | bytes 3145732
  2.4 48.3 %collective-permute-start.4 = (bf16[16,16,128]{2,1,0:T(8,128)(2,1)}, bf16[16,16,128]{2,1,0:T(8,128)(2,1)S(1)}, u32[]{:S(2)}, u32[]{:S(2)}) collective-permute-start(bf16[16,16,128]{2,1,0:T(8,128)(2,1)} %get-tuple-element.27), channel_id=1, source_target_pairs={{0,9},{1,10},{2,11},{3,12},{4,13},{5,14},{6,15},{8,17},{9,18},{10,... | collective-permute-start | bytes 196616 | tf_op jit(solution)/shard_map/ppermute | solution.py:586
  8.3 46.1 %collective-permute-start.5 = (bf16[16,16,128]{2,1,0:T(8,128)(2,1)}, bf16[16,16,128]{2,1,0:T(8,128)(2,1)S(1)}, u32[]{:S(2)}, u32[]{:S(2)}) collective-permute-start(bf16[16,16,128]{2,1,0:T(8,128)(2,1)} %get-tuple-element.26), channel_id=1, source_target_pairs={{1,8},{2,9},{3,10},{4,11},{5,12},{6,13},{7,14},{9,16},{10,17},{11,... | collective-permute-start | bytes 196616 | tf_op jit(solution)/shard_map/ppermute | solution.py:586
  10.6 54.7 %collective-permute-start.6 = (bf16[16,16,128]{2,1,0:T(8,128)(2,1)}, bf16[16,16,128]{2,1,0:T(8,128)(2,1)}, u32[]{:S(2)}, u32[]{:S(2)}) collective-permute-start(bf16[16,16,128]{2,1,0:T(8,128)(2,1)} %get-tuple-element.25), channel_id=1, source_target_pairs={{8,1},{9,2},{10,3},{11,4},{12,5},{13,6},{14,7},{16,9},{17,10},{18,... | collective-permute-start | bytes 196616 | tf_op jit(solution)/shard_map/ppermute | solution.py:586
  14.7 58.3 %all-to-all-start = ((f32[256,1,128]{2,1,0:T(1,128)}), f32[256,1,128]{2,1,0:T(1,128)S(1)}, u32[]{:S(2)}, u32[]{:S(2)}) async-start(f32[256,1,128]{2,1,0:T(1,128)} %bitcast.169), calls=%async_computation | async-start | bytes 262144 | tf_op jit(solution)/shard_map/all_to_all | solution.py:598
  31.9 6.6 %copy-start.9 = (bf16[3,3,128,3]{2,3,1,0:T(4,128)(2,1)S(1)}, bf16[3,3,128,3]{2,3,1,0:T(4,128)(2,1)}, u32[]{:S(2)}) copy-start(bf16[3,3,128,3]{2,3,1,0:T(4,128)(2,1)} %param.18) | copy-start | bytes 20740
  31.9 7.2 %copy-start.3 = (bf16[3,3,128,128]{3,2,1,0:T(8,128)(2,1)S(1)}, bf16[3,3,128,128]{3,2,1,0:T(8,128)(2,1)}, u32[]{:S(2)}) copy-start(bf16[3,3,128,128]{3,2,1,0:T(8,128)(2,1)} %param.26) | copy-start | bytes 884740
  33.0 40.0 %collective-permute-start = (bf16[16,128,128]{2,1,0:T(8,128)(2,1)}, bf16[16,128,128]{2,1,0:T(8,128)(2,1)}, u32[]{:S(2)}, u32[]{:S(2)}) collective-permute-start(bf16[16,128,128]{2,1,0:T(8,128)(2,1)} %get-tuple-element.31), channel_id=1, source_target_pairs={{0,8},{1,9},{2,10},{3,11},{4,12},{5,13},{6,14},{7,15},{8,16},{9,17... | collective-permute-start | bytes 1572872 | tf_op jit(solution)/shard_map/ppermute | solution.py:586
  37.2 35.8 %collective-permute-start.1 = (bf16[16,128,128]{2,1,0:T(8,128)(2,1)}, bf16[16,128,128]{2,1,0:T(8,128)(2,1)}, u32[]{:S(2)}, u32[]{:S(2)}) collective-permute-start(bf16[16,128,128]{2,1,0:T(8,128)(2,1)} %get-tuple-element.30), channel_id=1, source_target_pairs={{8,0},{9,1},{10,2},{11,3},{12,4},{13,5},{14,6},{15,7},{16,8},{17,9... | collective-permute-start | bytes 1572872 | tf_op jit(solution)/shard_map/ppermute | solution.py:586
  42.1 1.9 copy-start.20
  42.2 5.3 %copy-start.16 = (bf16[12,3,128,4]{2,3,1,0:T(4,128)(2,1)}, bf16[12,3,128,4]{2,3,1,0:T(4,128)(2,1)S(1)}, u32[]{:S(2)}) copy-start(bf16[12,3,128,4]{2,3,1,0:T(4,128)(2,1)S(1)} %constant_dynamic-update-slice_fusion) | copy-start | bytes 110596
  50.7 7.1 %copy-start.12 = (bf16[16,16,128]{2,1,0:T(8,128)(2,1)}, bf16[16,16,128]{2,1,0:T(8,128)(2,1)S(1)}, u32[]{:S(2)}) copy-start(bf16[16,16,128]{2,1,0:T(8,128)(2,1)S(1)} %collective-permute-done.4.r_7_) | copy-start | bytes 196612
  50.7 22.2 %collective-permute-start.2 = (bf16[32,16,128]{2,1,0:T(8,128)(2,1)S(1)}, bf16[32,16,128]{2,1,0:T(8,128)(2,1)S(1)}, u32[]{:S(2)}, u32[]{:S(2)}) collective-permute-start(bf16[32,16,128]{2,1,0:T(8,128)(2,1)S(1)} %get-tuple-element.29), channel_id=1, source_target_pairs={{0,1},{1,2},{2,3},{3,4},{4,5},{5,6},{6,7},{8,9},{9,10},{10,11},{11... | collective-permute-start | bytes 393224 | tf_op jit(solution)/shard_map/ppermute | solution.py:586
  54.5 3.4 %copy-start.13 = (bf16[16,16,128]{2,1,0:T(8,128)(2,1)}, bf16[16,16,128]{2,1,0:T(8,128)(2,1)S(1)}, u32[]{:S(2)}) copy-start(bf16[16,16,128]{2,1,0:T(8,128)(2,1)S(1)} %collective-permute-done.5.r_8_) | copy-start | bytes 196612
  54.5 18.5 %collective-permute-start.3 = (bf16[32,16,128]{2,1,0:T(8,128)(2,1)S(1)}, bf16[32,16,128]{2,1,0:T(8,128)(2,1)S(1)}, u32[]{:S(2)}, u32[]{:S(2)}) collective-permute-start(bf16[32,16,128]{2,1,0:T(8,128)(2,1)S(1)} %get-tuple-element.28), channel_id=1, source_target_pairs={{1,0},{2,1},{3,2},{4,3},{5,4},{6,5},{7,6},{9,8},{10,9},{11,10},{12... | collective-permute-start | bytes 393224 | tf_op jit(solution)/shard_map/ppermute | solution.py:586
  61.8 2.1 copy-start.26
  61.8 2.1 %copy-start.27 = (f32[128]{0:T(128)S(1)}, f32[128]{0:T(128)}, u32[]{:S(2)}) copy-start(f32[128]{0:T(128)} %param.25) | copy-start | bytes 1540
  61.8 2.1 %copy-start.28 = (f32[128]{0:T(128)S(1)}, f32[128]{0:T(128)}, u32[]{:S(2)}) copy-start(f32[128]{0:T(128)} %param.27) | copy-start | bytes 1540
  62.7 2.6 %copy-start.15 = (bf16[16,16,128]{2,1,0:T(8,128)(2,1)S(1)}, bf16[16,16,128]{2,1,0:T(8,128)(2,1)}, u32[]{:S(2)}) copy-start(bf16[16,16,128]{2,1,0:T(8,128)(2,1)} %get-tuple-element.24) | copy-start | bytes 196612
  65.3 7.7 %collective-permute-start.7 = (bf16[16,16,128]{2,1,0:T(8,128)(2,1)S(1)}, bf16[16,16,128]{2,1,0:T(8,128)(2,1)S(1)}, u32[]{:S(2)}, u32[]{:S(2)}) collective-permute-start(bf16[16,16,128]{2,1,0:T(8,128)(2,1)S(1)} %copy-done.15), channel_id=1, source_target_pairs={{9,0},{10,1},{11,2},{12,3},{13,4},{14,5},{15,6},{17,8},{18,9},{19,... | collective-permute-start | bytes 196616 | tf_op jit(solution)/shard_map/ppermute | solution.py:586
  114.9 26.8 %all-to-all-start.1 = ((f32[256,1,128]{2,1,0:T(1,128)}), f32[256,1,128]{2,1,0:T(1,128)S(1)}, u32[]{:S(2)}, u32[]{:S(2)}) async-start(f32[256,1,128]{2,1,0:T(1,128)} %bitcast.175), calls=%async_computation.1 | async-start | bytes 262144 | tf_op jit(solution)/shard_map/all_to_all | solution.py:598
  142.7 5.9 %copy-start.19 = (bf16[12,3,64,4]{2,3,1,0:T(4,128)(2,1)S(1)}, bf16[12,3,64,4]{2,3,1,0:T(4,128)(2,1)}, u32[]{:S(2)}) copy-start(bf16[12,3,64,4]{2,3,1,0:T(4,128)(2,1)} %copy-done.18) | copy-start | bytes 55300
  142.7 18.9 %all-to-all-start.2 = ((f32[256,1,128]{2,1,0:T(1,128)}), f32[256,1,128]{2,1,0:T(1,128)S(1)}, u32[]{:S(2)}, u32[]{:S(2)}) async-start(f32[256,1,128]{2,1,0:T(1,128)} %reshape.85), calls=%async_computation.2 | async-start | bytes 262144 | tf_op jit(solution)/shard_map/all_to_all | solution.py:598
  182.0 22.8 %all-to-all-start.3 = ((f32[256,1,128]{2,1,0:T(1,128)}), f32[256,1,128]{2,1,0:T(1,128)S(1)}, u32[]{:S(2)}, u32[]{:S(2)}) async-start(f32[256,1,128]{2,1,0:T(1,128)} %bitcast.176), calls=%async_computation.3 | async-start | bytes 262144 | tf_op jit(solution)/shard_map/all_to_all | solution.py:598
  (17 other events, 13.0 us)
